TPU v7x, 256 devices: a whole 4x4x8 slice. The times are simulated.
256 devices in a mesh: freq: 32 (over z, x), brow: 2 (over y_hi), bcol: 4 (over y_lo, core).
Axes of the slice: x: 4, y: 4 (y_hi: 2, y_lo: 2; y = y_hi * 2 + y_lo), z: 8, core: 2. Of those that a mesh axis runs over, the one named last changes fastest.
Arguments:
- voltages: bfloat16 [2, 1024, 94208], P(None, ('brow', 'bcol', 'freq')), may hold values from -6 to 6
- fir_taps: float32 [16, 4096], replicated, may hold values from -1.5 to 1.5
Outputs:
- visibilities: float32 [2, 128, 1024, 2, 4, 128], P(None, 'freq', 'brow', None, 'bcol')
All inputs are finite; a program needn't handle non-finite values.
Results may differ from a plain program's by a relative error of at most 0.0036.
Values may be sent and summed in bfloat16 or wider, within the bound.
A program may use at most 64 MiB of HBM per device.

v0:
```python
import math

import jax
import jax.numpy as jnp
from jax import lax
from jax.sharding import PartitionSpec as P

CHANNELS = 4096
RADIX = 64
TAPS = 16
AVG = 32
FRAMES = 8


def dft_table(length):
    index = jnp.arange(length, dtype=jnp.int32)
    phase = index[:, None] * index[None, :] % length
    angle = phase.astype(jnp.float32) * (2.0 * math.pi / length)
    cosine = jnp.cos(angle)
    sine = jnp.sin(angle)
    return jnp.stack([jnp.stack([cosine, sine]), jnp.stack([-sine, cosine])])


def channelize(voltages, fir_taps, first, count):
    width = voltages.shape[1]
    frames = voltages.reshape(2, width, FRAMES + TAPS - 1, CHANNELS)

    def add_tap(tap, filtered):
        window = lax.dynamic_slice_in_dim(frames, first + tap, count, 2).astype(jnp.float32)
        return filtered + fir_taps[tap] * window

    filtered = lax.fori_loop(0, TAPS, add_tap, jnp.zeros((2, width, count, CHANNELS), jnp.float32))
    stacked = filtered.reshape(2, width, count, RADIX, RADIX)
    table = dft_table(RADIX)
    section = jnp.einsum("cwtbn,dcbk->dwtkn", stacked, table, precision=lax.Precision.HIGHEST)
    index = jnp.arange(RADIX, dtype=jnp.int32)
    phase = (index[:, None] * index[None, :]).astype(jnp.float32) * (2.0 * math.pi / CHANNELS)
    tw_cos = jnp.cos(phase)
    tw_sin = jnp.sin(phase)
    turned = jnp.stack(
        [section[0] * tw_cos + section[1] * tw_sin, section[1] * tw_cos - section[0] * tw_sin]
    )
    spectrum = jnp.einsum("cwtkn,dcnm->dwtmk", turned, table, precision=lax.Precision.HIGHEST) * (
        1.0 / RADIX
    )
    return spectrum.astype(jnp.bfloat16).reshape(2, width, count, CHANNELS)


def shards(voltages, fir_taps):
    local = channelize(voltages, fir_taps, 0, FRAMES)
    owned = lax.all_to_all(local, "freq", split_axis=3, concat_axis=1, tiled=True)
    group = owned.shape[3]
    coarse = group // AVG
    scale = 1.0 / (FRAMES * AVG)
    block = owned.shape[1]
    row_count = lax.axis_size("brow")
    col_block = lax.all_gather(owned, "brow", axis=1, tiled=True)
    left_rows = lax.all_gather(owned, "bcol", axis=1, tiled=True)
    left = left_rows.reshape(2, left_rows.shape[1], FRAMES, coarse, AVG)
    right = col_block.reshape(2, col_block.shape[1], FRAMES, coarse, AVG)
    flipped = jnp.stack([-right[1], right[0]])
    real_part = jnp.einsum("cptqa,cutqa->qpu", left, right, preferred_element_type=jnp.float32)
    imag_part = jnp.einsum("cptqa,cutqa->qpu", left, flipped, preferred_element_type=jnp.float32)
    result = jnp.stack([real_part, imag_part]) * scale
    return result.reshape(2, coarse, result.shape[2], row_count, 1, block)


def solution(mesh):
    in_specs = (P(None, ("brow", "bcol", "freq"), None), P())
    out_specs = P(None, "freq", "brow", None, "bcol", None)
    return jax.shard_map(shards, mesh=mesh, in_specs=in_specs, out_specs=out_specs, check_vma=False)
```

profile of v0, /device:TPU:2, one launch (start us, length us, event | category | flops | bytes accessed | tf_op | source)
XLA Modules:
  0.0 200.2 jit_solution(7456410314755574739)
XLA Ops:
  7.0 2.1 %reshape.165 = bf16[2,4,23,4096]{3,2,1,0:T(8,128)(2,1)S(1)} reshape(bf16[2,4,94208]{2,1,0:T(4,128)(2,1)} %param.4) | data formatting | bytes 3014656 | tf_op jit(solution)/shard_map/reshape | solution.py:26
  9.1 23.2 %while.14 = (s32[]{:T(128)}, f32[2,4,8,4096]{3,2,1,0:T(8,128)S(1)}, f32[16,4096]{1,0:T(8,128)}, bf16[2,4,23,4096]{3,2,1,0:T(8,128)(2,1)S(1)}, s32[]{:T(128)}, /*index=5*/s32[]{:T(128)}) while((s32[]{:T(128)}, f32[2,4,8,4096]{3,2,1,0:T(8,128)S(1)}, f32[16,4096]{1,0:T(8,128)}, bf16[2,4,23,4096]{3,2,1,0:T(8,128)(2,1)S(1)}, s32[]{:T(128)}, ...), condition=%wide.region_1.0_spmd.clone, body=%wide.region_0.0_spmd.clone.sunk | while | flops 1048579 | bytes 2670687 | solution.py:32
  16.4 0.9 constant_dynamic-slice_fusion.2
  17.8 0.9 constant_dynamic-slice_fusion.2
  19.3 0.9 constant_dynamic-slice_fusion.2
  20.7 0.9 constant_dynamic-slice_fusion.2
  33.2 2.0 fusion.7
  35.6 3.1 %fusion.12 = bf16[2,4,8,64,64]{4,3,2,1,0:T(8,128)(2,1)S(1)} fusion(f32[1,2,64,64]{2,3,1,0:T(8,128)S(1)} %get-tuple-element.113, f32[1,2,64,64]{2,3,1,0:T(8,128)S(1)} %get-tuple-element.112, f32[1,4,8,64,64]{4,3,2,1,0:T(8,128)S(1)} %get-tuple-element.109, f32[1,4,8,64,64]{4,3,2,1,0:T(8,128)S(1)} %get-tuple-element.108), kind=kOutput, calls=%fused_computation.13 | convolution fusion | flops 403456000 | bytes 1638400 | tf_op jit(solution)/shard_map/cwtkn,dcnm->dwtmk/dot_general | solution.py:43
  38.7 9.3 %copy.45 = bf16[2,4,8,64,64]{2,1,0,4,3:T(4,128)(2,1)} copy(bf16[2,4,8,64,64]{4,3,2,1,0:T(8,128)(2,1)S(1)} %fusion.12) | data formatting | bytes 1048576 | tf_op jit(solution)/shard_map/reshape | solution.py:46
  48.0 10.5 %reshape.177 = bf16[32,2,4096]{2,1,0:T(2,128)(2,1)S(1)} reshape(bf16[4096,2,4,8]{3,2,1,0:T(4,128)(2,1)} %bitcast.66) | data formatting | bytes 1048576
  58.5 28.2 %all_to_all.18 = bf16[32,2,4096]{2,1,0:T(2,128)(2,1)S(1)} all-to-all(bf16[32,2,4096]{2,1,0:T(2,128)(2,1)S(1)} %reshape.177), channel_id=1, replica_groups=mesh['freq'=32,'brow'=2,'bcol'=4] {'freq'}, dimensions={0} | all-to-all | bytes 1048576 | tf_op jit(solution)/shard_map/all_to_all | solution.py:51
  86.7 10.9 %reshape.178 = bf16[4096,2,4,8]{3,2,1,0:T(4,128)(2,1)} reshape(bf16[32,2,4096]{2,1,0:T(2,128)(2,1)S(1)} %all_to_all.18) | data formatting | bytes 1048576
  97.7 10.6 %copy.47 = bf16[2,4,8,32,128]{4,2,1,3,0:T(8,128)(2,1)} copy(bf16[2,4,8,32,128]{2,1,0,4,3:T(4,128)(2,1)} %bitcast.67) | data formatting | bytes 1048576 | tf_op jit(solution)/shard_map/all_to_all | solution.py:51
  109.0 24.2 %all-gather.5.cloned.1.call-done = bf16[2,256,8,128]{3,2,1,0:T(8,128)(2,1)} async-done(((bf16[2,128,8,128]{3,2,1,0:T(8,128)(2,1)}), bf16[2,256,8,128]{3,2,1,0:T(8,128)(2,1)}) %all-gather.5.cloned.1.call-update) | async-done | bytes 1048592 | tf_op jit(solution)/shard_map/all_gather | solution.py:57
  133.2 1.4 slice_negate_fusion
  134.6 1.1 copy.36
  135.7 1.1 copy.37
  137.6 28.4 %all-gather.3.cloned.1.call-done = bf16[2,512,8,128]{3,2,1,0:T(8,128)(2,1)} async-done(((bf16[2,128,8,128]{3,2,1,0:T(8,128)(2,1)}), bf16[2,512,8,128]{3,2,1,0:T(8,128)(2,1)}) %all-gather.3.cloned.1.call-update) | async-done | bytes 2097168 | tf_op jit(solution)/shard_map/all_gather | solution.py:58
  166.0 3.0 %copy.34 = bf16[2,512,8,128]{1,3,2,0:T(8,128)(2,1)S(1)} copy(bf16[2,512,8,128]{3,2,1,0:T(8,128)(2,1)} %all-gather.3.cloned.1.call-done) | data formatting | bytes 4194304 | tf_op jit(solution)/shard_map/all_gather | solution.py:58
  169.0 2.1 %fusion.33 = f32[4,512,256,1,1]{1,2,0,4,3:T(8,128)} fusion(bf16[2,512,8,4,32]{1,4,3,2,0:T(8,128)(2,1)S(1)} %bitcast.68, bf16[2,256,8,4,32]{1,4,3,2,0:T(8,128)(2,1)S(1)} %bitcast.74), kind=kOutput, calls=%fused_computation.42 | convolution fusion | flops 536870912 | bytes 5242880 | tf_op jit(solution)/shard_map/cptqa,cutqa->qpu/dot_general | solution.py:62
  171.1 6.1 %copy.38 = f32[1,4,512,2,1,128]{5,4,3,2,1,0:T(1,128)} copy(f32[1,4,512,2,1,128]{2,5,3,1,4,0:T(8,128)} %bitcast.71) | data formatting | bytes 4194304 | tf_op jit(solution)/shard_map/stack | solution.py:64
  177.2 2.1 %fusion.15 = f32[4,512,256,1,1]{1,2,0,4,3:T(8,128)} fusion(bf16[2,512,8,4,32]{1,4,3,2,0:T(8,128)(2,1)S(1)} %bitcast.69, bf16[1,256,8,4,32]{1,4,3,2,0:T(8,128)(2,1)S(1)} %bitcast.76, bf16[1,256,8,4,32]{1,4,3,2,0:T(8,128)(2,1)S(1)} %bitcast.75), kind=kOutput, calls=%fused_computation.14 | convolution fusion | flops 537395200 | bytes 5242880 | tf_op jit(solution)/shard_map/cptqa,cutqa->qpu/dot_general | solution.py:63
  179.3 6.2 %copy.39 = f32[1,4,512,2,1,128]{5,4,3,2,1,0:T(1,128)} copy(f32[1,4,512,2,1,128]{2,5,3,1,4,0:T(8,128)} %bitcast.70) | data formatting | bytes 4194304 | tf_op jit(solution)/shard_map/stack | solution.py:64
  185.5 7.9 %maximum_multiply_fusion = f32[2,4,512,2,1,128]{5,4,3,2,1,0:T(1,128)} fusion(f32[1,4,512,2,1,128]{5,4,3,2,1,0:T(1,128)} %copy.39, f32[1,4,512,2,1,128]{5,4,3,2,1,0:T(1,128)S(1)} %copy-done), kind=kLoop, calls=%fused_computation.2 | loop fusion | flops 2097152 | bytes 8388608 | tf_op jit(solution)/shard_map/mul | solution.py:64
  (48 shorter events, 22.2 us)
Async XLA Ops:
  6.5 126.7 %all-gather.5.cloned.1.call-start = ((), (), s32[]{:S(2)}) async-start(), calls=%async_computation.2 | async-start | bytes 1572864 | tf_op jit(solution)/shard_map/all_gather | solution.py:57
  108.2 57.7 %all-gather.3.cloned.1.call-start = ((), (), s32[]{:S(2)}) async-start(), calls=%async_computation.1 | async-start | bytes 2621440 | tf_op jit(solution)/shard_map/all_gather | solution.py:58
  133.2 3.7 %copy-start.1 = (bf16[2,256,8,128]{3,2,1,0:T(8,128)(2,1)S(1)}, bf16[2,256,8,128]{3,2,1,0:T(8,128)(2,1)}, u32[]{:S(2)}) copy-start(bf16[2,256,8,128]{3,2,1,0:T(8,128)(2,1)} %all-gather.5.cloned.1.call-done) | copy-start | bytes 3145732
  171.1 6.2 %copy-start.2 = (bf16[1,256,8,128]{1,3,2,0:T(8,128)(2,1)S(1)}, bf16[1,256,8,128]{1,3,2,0:T(8,128)(2,1)}, u32[]{:S(2)}) copy-start(bf16[1,256,8,128]{1,3,2,0:T(8,128)(2,1)} %copy.36) | copy-start | bytes 1572868
  171.1 6.2 %copy-start.3 = (bf16[1,256,8,128]{1,3,2,0:T(8,128)(2,1)S(1)}, bf16[1,256,8,128]{1,3,2,0:T(8,128)(2,1)}, u32[]{:S(2)}) copy-start(bf16[1,256,8,128]{1,3,2,0:T(8,128)(2,1)} %copy.37) | copy-start | bytes 1572868
  179.3 6.2 %copy-start = (f32[1,4,512,2,1,128]{5,4,3,2,1,0:T(1,128)S(1)}, f32[1,4,512,2,1,128]{5,4,3,2,1,0:T(1,128)}, u32[]{:S(2)}) copy-start(f32[1,4,512,2,1,128]{5,4,3,2,1,0:T(1,128)} %copy.38) | copy-start | bytes 6291460
Sparse Core Ops, SparseCore 0:
  108.4 24.8 all-gather.4
  135.0 30.9 all-gather.2
where the time goes:
time: 203 us; the launch traced here: 200 us
  local copies, waits for them, and re-layouts  77.2 us (38%)
  waiting for transfers between devices  53.2 us (26%)
  blocking collectives  28.2 us (14%)
  other arithmetic  18.2 us (9%)
  between operations  13.5 us (7%)
  matrix products  9.25 us (5%)
    all_gather x1, waiting for transfers between devices, shards(): left_rows = lax.all_gather(owned, 'bcol', axis=1, tiled=True)  28.4 us
    all_to_all x1, blocking collectives, shards(): lax.all_to_all(local, 'freq', split_axis=3, concat_axis=1, tiled=True)  28.2 us
    all_gather x1, waiting for transfers between devices, shards(): col_block = lax.all_gather(owned, 'brow', axis=1, tiled=True)  24.2 us
    unnamed x10, local copies, waits for them, and re-layouts  21.4 us
    dynamic_slice x16, local copies, waits for them, and re-layouts, add_tap(): return filtered + fir_taps[tap] * window  14.8 us
    another operation x2, local copies, waits for them, and re-layouts, shards(): result = jnp.stack([real_part, imag_part]) * scale  12.3 us
    all_to_all x1, local copies, waits for them, and re-layouts, shards(): lax.all_to_all(local, 'freq', split_axis=3, concat_axis=1, tiled=True)  10.6 us
    reshape x1, local copies, waits for them, and re-layouts, channelize(): return spectrum.astype(jnp.bfloat16).reshape(2, width, count, CHANNELS)  9.33 us
  transfers between devices with their start and end apart: 2, of which 2 were waited for; matrix products, arithmetic and copies ran while one was open for 2% of the time, Pallas kernels for 0%

commit v1 on v0

v1 whole, which is shorter than its diff:
```python
import functools
import math

import jax
import jax.numpy as jnp
import numpy as np
from jax import lax
from jax.experimental import pallas as pl
from jax.experimental.pallas import tpu as pltpu
from jax.sharding import PartitionSpec as P

CHANNELS = 4096
SCALE = 1.0 / 64.0
TAPS = 16
AVG = 32
FRAMES = 8
SLOW = 32
FAST = 128
WIDTH = 4
OWNED = 4
GROUPS = 32
KEPT = FRAMES * SLOW
ROWS = 2 * WIDTH
F32 = jnp.float32
BF16 = jnp.bfloat16


def halves(table):
    high = table.astype(np.float32).astype(jnp.bfloat16)
    low = (table - high.astype(np.float64)).astype(np.float32).astype(jnp.bfloat16)
    return high, low


def tables():
    b, k1 = np.arange(SLOW), np.arange(SLOW)
    angle = 2.0 * np.pi * (np.outer(k1, b) % SLOW) / SLOW
    first = np.zeros((2, WIDTH, SLOW, SLOW, 2, WIDTH))
    for s in range(WIDTH):
        first[0, s, :, :, 0, s] = np.cos(angle)
        first[0, s, :, :, 1, s] = np.sin(angle)
        first[1, s, :, :, 0, s] = -np.sin(angle)
        first[1, s, :, :, 1, s] = np.cos(angle)
    first = first.reshape(256, 256)
    n, m = np.arange(FAST), np.arange(FAST)
    angle = 2.0 * np.pi * (np.outer(m, n) % FAST) / FAST
    second = np.zeros((FAST, 2, 2, FAST))
    second[:, 0, 0, :] = np.cos(angle)
    second[:, 0, 1, :] = np.sin(angle)
    second[:, 1, 0, :] = -np.sin(angle)
    second[:, 1, 1, :] = np.cos(angle)
    second = second.reshape(256, 256) * SCALE
    angle = 2.0 * np.pi * np.outer(k1, n) / CHANNELS
    turn = np.stack([np.cos(angle), np.sin(angle)]).astype(np.float32)
    sort = np.zeros((2, GROUPS, WIDTH, GROUPS, 2, WIDTH), np.float32)
    for d in range(2):
        for g in range(GROUPS):
            for s in range(WIDTH):
                sort[d, g, s, g, d, s] = 1.0
    sort = sort.reshape(256, 256).astype(jnp.bfloat16)
    return np.stack(halves(first)), np.stack(halves(second)), turn, sort


FIRST, SECOND, TURN, SORT = tables()
NT = (((1,), (1,)), ((), ()))


def split(value):
    high = value.astype(BF16)
    low = (value - high.astype(F32)).astype(BF16)
    return high, low


def channelize_kernel(x_ref, taps_ref, first_ref, second_ref, turn_ref, out_ref, fir, spread):
    def column(b, carry):
        lanes = pl.multiple_of(b * FAST, FAST)
        rows = pl.multiple_of(b * ROWS, ROWS)
        frames = []
        for j in range(FRAMES + TAPS - 1):
            at = pl.multiple_of(j * CHANNELS + lanes, FAST)
            real = x_ref[0, :, pl.ds(at, FAST)].astype(F32)
            imag = x_ref[1, :, pl.ds(at, FAST)].astype(F32)
            frames.append(jnp.concatenate([real, imag], axis=0))
        taps = [taps_ref[pl.ds(p, 1), pl.ds(lanes, FAST)] for p in range(TAPS)]
        for t in range(FRAMES):
            total = taps[0] * frames[t]
            for p in range(1, TAPS):
                total = total + taps[p] * frames[t + p]
            fir[pl.ds(rows, ROWS), t * FAST:(t + 1) * FAST] = total
        return carry

    lax.fori_loop(0, SLOW, column, 0)
    high, low = split(fir[...])
    dot = functools.partial(jnp.dot, preferred_element_type=F32)
    section = dot(first_ref[0], high) + dot(first_ref[1], high) + dot(first_ref[0], low)
    cosine, sine = turn_ref[0], turn_ref[1]
    for s in range(WIDTH):
        parts = []
        for t in range(FRAMES):
            real = section[s * SLOW:(s + 1) * SLOW, t * FAST:(t + 1) * FAST]
            imag = section[128 + s * SLOW:128 + (s + 1) * SLOW, t * FAST:(t + 1) * FAST]
            parts.append(jnp.concatenate([real * cosine + imag * sine, imag * cosine - real * sine], axis=1))
        high, low = split(jnp.concatenate(parts, axis=0))
        dot_nt = functools.partial(lax.dot_general, dimension_numbers=NT, preferred_element_type=F32)
        spectrum = dot_nt(second_ref[0], high) + dot_nt(second_ref[1], high) + dot_nt(second_ref[0], low)
        for half in range(2):
            lanes = slice(half * 128, (half + 1) * 128)
            spread[half, pl.ds(s, 256, stride=WIDTH), :] = spectrum[:, lanes]
    for half in range(2):
        out_ref[:, half * 128:(half + 1) * 128] = spread[half].astype(BF16)


def channelize(voltages, fir_taps):
    vmem = pl.BlockSpec(memory_space=pltpu.VMEM)
    return pl.pallas_call(
        channelize_kernel,
        out_shape=jax.ShapeDtypeStruct((GROUPS * OWNED * ROWS, KEPT), BF16),
        in_specs=[vmem] * 5,
        out_specs=vmem,
        scratch_shapes=[
            pltpu.VMEM((256, FRAMES * FAST), F32),
            pltpu.VMEM((2, GROUPS * OWNED * ROWS, 128), F32),
        ],
        name="channelize",
    )(voltages, fir_taps, jnp.asarray(FIRST), jnp.asarray(SECOND), jnp.asarray(TURN))


def correlate_kernel(slots_ref, left_ref, first_ref, second_ref, sort_ref, out_ref):
    del slots_ref
    sort = sort_ref[...]
    sorted_blocks = [
        jnp.dot(sort, ref[0, 0], preferred_element_type=F32).astype(BF16) for ref in (first_ref, second_ref)
    ]
    right = jnp.concatenate(
        [sorted_blocks[0][:128], sorted_blocks[1][:128], sorted_blocks[0][128:], sorted_blocks[1][128:]], axis=0
    )
    upper = lax.broadcasted_iota(jnp.int32, (GROUPS, ROWS, 256), 1) < WIDTH
    for block in range(left_ref.shape[0]):
        product = lax.dot_general(left_ref[block, 0], right, NT, preferred_element_type=F32)
        with_real = product[:, :256].reshape(GROUPS, ROWS, 256)
        with_imag = pltpu.roll(product[:, 256:].reshape(GROUPS, ROWS, 256), WIDTH, axis=1)
        mixed = (with_real + jnp.where(upper, with_imag, -with_imag)) * (1.0 / (FRAMES * AVG))
        pairs = mixed.reshape(GROUPS // 2, 2, ROWS, 256)
        even, odd = pairs[:, 0], pairs[:, 1]
        real = jnp.where(upper[:GROUPS // 2], even, pltpu.roll(odd, WIDTH, axis=1)).reshape(128, 256)
        imag = jnp.where(upper[:GROUPS // 2], pltpu.roll(even, WIDTH, axis=1), odd).reshape(128, 256)
        for r in range(2):
            rows = pl.ds(block * 256 + r, 128, stride=2)
            out_ref[0, 0, rows, :] = real[:, r * 128:(r + 1) * 128]
            out_ref[1, 0, rows, :] = imag[:, r * 128:(r + 1) * 128]


def correlate(blocks, slots):
    grid_spec = pltpu.PrefetchScalarGridSpec(
        num_scalar_prefetch=1,
        grid=(OWNED,),
        in_specs=[
            pl.BlockSpec((4, 1, 256, KEPT), lambda q, slots: (0, q, 0, 0)),
            pl.BlockSpec((1, 1, 256, KEPT), lambda q, slots: (slots[0], q, 0, 0)),
            pl.BlockSpec((1, 1, 256, KEPT), lambda q, slots: (slots[1], q, 0, 0)),
            pl.BlockSpec((256, 256), lambda q, slots: (0, 0)),
        ],
        out_specs=pl.BlockSpec((2, 1, 1024, 128), lambda q, slots: (0, q, 0, 0)),
    )
    return pl.pallas_call(
        correlate_kernel,
        grid_spec=grid_spec,
        out_shape=jax.ShapeDtypeStruct((2, OWNED, 1024, 128), F32),
        name="correlate",
    )(slots, blocks, blocks, blocks, jnp.asarray(SORT))


def exchange(spectra):
    owned = lax.all_to_all(spectra.reshape(GROUPS, OWNED, ROWS, KEPT), "freq", split_axis=0, concat_axis=0, tiled=True)
    owned = owned.transpose(1, 0, 2, 3).reshape(OWNED, 256, KEPT)
    left = lax.all_gather(owned, "bcol", axis=0)
    right = lax.all_gather(owned, "brow", axis=0)
    other = lax.dynamic_index_in_dim(right, 1 - lax.axis_index("brow"), 0)
    return jnp.concatenate([left, other], axis=0)


def shards(voltages, fir_taps):
    spectra = channelize(voltages, fir_taps)
    blocks = exchange(spectra)
    brow, bcol = lax.axis_index("brow"), lax.axis_index("bcol")
    slots = jnp.stack([bcol + brow * (4 - bcol), 4 - brow * (4 - bcol)]).astype(jnp.int32)
    result = correlate(blocks, slots)
    return result.reshape(2, OWNED, 512, 2, 1, 128)


def solution(mesh):
    in_specs = (P(None, ("brow", "bcol", "freq"), None), P())
    out_specs = P(None, "freq", "brow", None, "bcol", None)
    return jax.shard_map(shards, mesh=mesh, in_specs=in_specs, out_specs=out_specs, check_vma=False)
```

time: 203 us -> 118 us (0.58)
  local copies, waits for them, and re-layouts: 77.2 us -> 1.9 us
  other arithmetic: 18.2 us -> 3.93 us
  Pallas kernels: 0 us -> 12.2 us
  matrix products: 9.25 us -> 0 us
  waiting for transfers between devices: 53.2 us -> 56 us
    unnamed x10 -> x0, local copies, waits for them, and re-layouts: 21.4 us -> none
    dynamic_slice x16 -> x1, local copies, waits for them, and re-layouts: 14.8 us -> 1.08 us  [exchange(): other = lax.dynamic_index_in_dim(right, 1 - lax.axis_index('brow'), 0)]
    another operation x2 -> x0, local copies, waits for them, and re-layouts: 12.3 us -> none  [shards(): result = jnp.stack([real_part, imag_part]) * scale]
    reshape x3 -> x0, local copies, waits for them, and re-layouts: 12.3 us -> none  [the longest x1 9.33 us: channelize(): return spectrum.astype(jnp.bfloat16).reshape(2, width, count, CHANNELS)]
    pallas_call x0 -> x2, Pallas kernels: none -> 12.2 us  [the longest x1 6.42 us: correlate(): pl.pallas_call(correlate_kernel, grid_spec=grid_spec, out_shape=jax.Shape...]
    all_to_all x1, local copies, waits for them, and re-layouts: 10.6 us -> 0.83 us  [exchange(): lax.all_to_all(spectra.reshape(GROUPS, OWNED, ROWS, KEPT), 'freq', split_...]
    dot_general x4 -> x0, matrix products: 9.25 us -> none  [the longest x1 3.13 us: channelize(): jnp.einsum('cwtkn,dcnm->dwtmk', turned, table, precision=lax.Precision.HI...]
    add x17 -> x0, other arithmetic: 8.47 us -> none  [the longest x16 8.05 us: add_tap(): return filtered + fir_taps[tap] * window]
  transfers between devices with their start and end apart: 2 -> 2, of which waited for: 2 -> 2; matrix products, arithmetic and copies ran while one was open for 2% -> 1% of each run, Pallas kernels for 0% -> 0%
where the time goes in v1:
time: 118 us; the launch traced here: 116 us
  waiting for transfers between devices  56 us (47%)
  blocking collectives  28.4 us (24%)
  between operations  13.4 us (11%)
  Pallas kernels  12.2 us (10%)
  other arithmetic  3.93 us (3%)
  local copies, waits for them, and re-layouts  1.9 us (2%)
    all_gather x1, waiting for transfers between devices, exchange(): left = lax.all_gather(owned, 'bcol', axis=0)  31.7 us
    all_to_all x1, blocking collectives, exchange(): lax.all_to_all(spectra.reshape(GROUPS, OWNED, ROWS, KEPT), 'freq', split_...  28.4 us
    all_gather x1, waiting for transfers between devices, exchange(): right = lax.all_gather(owned, 'brow', axis=0)  23.6 us
    pallas_call x1, Pallas kernels, correlate(): pl.pallas_call(correlate_kernel, grid_spec=grid_spec, out_shape=jax.Shape...  6.42 us
    pallas_call x1, Pallas kernels, channelize(): pl.pallas_call(channelize_kernel, out_shape=jax.ShapeDtypeStruct((GROUPS...  5.74 us
    concatenate x1, other arithmetic, exchange(): return jnp.concatenate([left, other], axis=0)  3.33 us
  transfers between devices with their start and end apart: 2, of which 2 were waited for; matrix products, arithmetic and copies ran while one was open for 1% of the time, Pallas kernels for 0%

profile of v1, /device:TPU:2, one launch (start us, length us, event | category | flops | bytes accessed | tf_op | source)
XLA Modules:
  0.0 115.9 jit_solution(11261880785672889990)
XLA Ops:
  6.5 0.0 all-gather.5.cloned.1.call-start
  6.5 5.7 %channelize.1 = bf16[1024,256]{1,0:T(8,128)(2,1)} custom-call(bf16[2,4,94208]{2,1,0:T(4,128)(2,1)} %x_ref.1, f32[16,4096]{1,0:T(8,128)} %taps_ref.1, bf16[2,256,256]{2,1,0:T(8,128)(2,1)} %constant.28.clone.first_ref, bf16[2,256,256]{2,1,0:T(8,128)(2,1)} %constant.29.clone.second_ref, f32[2,32,128]{2,1,0:T(8,128)} %constant.30.clone.turn_ref), custom_call_target="tpu_custom_call" | custom-call | tf_op jit(solution)/shard_map/channelize/pallas_call | solution.py:114
  12.3 28.4 %all_to_all.5 = bf16[32,4,8,256]{3,2,1,0:T(8,128)(2,1)S(1)} all-to-all(bf16[32,4,8,256]{3,2,1,0:T(8,128)(2,1)} %bitcast.13), channel_id=1, replica_groups=mesh['freq'=32,'brow'=2,'bcol'=4] {'freq'}, dimensions={0} | all-to-all | bytes 1048576 | tf_op jit(solution)/shard_map/all_to_all | solution.py:173
  40.7 0.8 copy.13
  41.5 0.0 all-gather.5.cloned.1.call-update
  41.6 0.0 all-gather.3.cloned.1.call-start
  41.6 0.7 all-gather.3.cloned.1.call-update
  42.3 0.6 pad_add_fusion.slots_ref
  42.9 23.6 %all-gather.5.cloned.1.call-done = bf16[2,4,256,256]{3,2,1,0:T(8,128)(2,1)} async-done(((bf16[1,4,256,256]{3,2,1,0:T(8,128)(2,1)}), bf16[2,4,256,256]{3,2,1,0:T(8,128)(2,1)}) %all-gather.5.cloned.1.call-update) | async-done | bytes 1048592 | tf_op jit(solution)/shard_map/all_gather | solution.py:176
  66.5 1.1 constant_dynamic-slice_fusion
  67.6 31.7 %all-gather.3.cloned.1.call-done = bf16[4,4,256,256]{3,2,1,0:T(8,128)(2,1)} async-done(((bf16[1,4,256,256]{3,2,1,0:T(8,128)(2,1)}), bf16[4,4,256,256]{3,2,1,0:T(8,128)(2,1)}) %all-gather.3.cloned.1.call-update) | async-done | bytes 2097168 | tf_op jit(solution)/shard_map/all_gather | solution.py:175
  99.3 3.3 %pad_maximum_fusion.left_ref.first_ref.second_ref = bf16[5,4,256,256]{3,2,1,0:T(8,128)(2,1)} fusion(bf16[1,4,256,256]{3,2,1,0:T(8,128)(2,1)S(1)} %constant_dynamic-slice_fusion, bf16[4,4,256,256]{3,2,1,0:T(8,128)(2,1)} %all-gather.3.cloned.1.call-done), kind=kLoop, calls=%fused_computation | loop fusion | flops 1310720 | bytes 5242880 | tf_op jit(solution)/shard_map/concatenate | solution.py:178
  102.6 6.4 %correlate.1 = f32[2,4,1024,128]{3,2,1,0:T(8,128)} custom-call(s32[2]{0:T(128)} %pad_add_fusion.slots_ref, bf16[5,4,256,256]{3,2,1,0:T(8,128)(2,1)} %pad_maximum_fusion.left_ref.first_ref.second_ref, bf16[5,4,256,256]{3,2,1,0:T(8,128)(2,1)} %pad_maximum_fusion.left_ref.first_ref.second_ref, ...), custom_call_target="tpu_custom_call" | custom-call | tf_op jit(solution)/shard_map/correlate/pallas_call | solution.py:164
Async XLA Ops:
  6.5 60.0 %all-gather.5.cloned.1.call-start = ((), (), s32[]{:S(2)}) async-start(), calls=%async_computation.2 | async-start | bytes 1572864 | tf_op jit(solution)/shard_map/all_gather | solution.py:176
  41.6 57.7 %all-gather.3.cloned.1.call-start = ((), (), s32[]{:S(2)}) async-start(), calls=%async_computation.1 | async-start | bytes 2621440 | tf_op jit(solution)/shard_map/all_gather | solution.py:175
Sparse Core Ops, SparseCore 0:
  41.7 24.8 all-gather.4
  68.4 30.9 all-gather.2

commit v2 on v1

--- a/solution.py
+++ b/solution.py
@@ -21,6 +21,10 @@
 GROUPS = 32
 KEPT = FRAMES * SLOW
 ROWS = 2 * WIDTH
+N_X = 4
+N_Z = 8
+N_BCOL = 4
+MESH = pl.DeviceIdType.MESH
 F32 = jnp.float32
 BF16 = jnp.bfloat16
 
@@ -169,13 +173,101 @@
     )(slots, blocks, blocks, blocks, jnp.asarray(SORT))
 
 
+def exchange_kernel(
+    spectra, blocks, local, turn_send, turn_recv, near_send, core_send, relay_send, far_send, near_recv, core_recv,
+    relay_recv, far_recv
+):
+    freq, brow, bcol = lax.axis_index("freq"), lax.axis_index("brow"), lax.axis_index("bcol")
+    z, x = freq // N_X, freq % N_X
+    y_low, core = bcol // 2, bcol % 2
+    other_core = 2 * y_low + 1 - core
+    near = 2 * (1 - y_low) + core
+
+    barrier = pltpu.get_barrier_semaphore()
+
+    def greet(i, carry):
+        pl.semaphore_signal(barrier, inc=1, device_id=((freq + i) % GROUPS, brow, bcol), device_id_type=MESH)
+        return carry
+
+    lax.fori_loop(1, GROUPS, greet, 0)
+    for peer in ((freq, brow, other_core), (freq, brow, near), (freq, 1 - brow, near)):
+        pl.semaphore_signal(barrier, inc=1, device_id=peer, device_id_type=MESH)
+    pl.semaphore_wait(barrier, GROUPS - 1 + 3)
+
+    def shift(j):
+        return (N_Z + ((j + 1) // 2) * (2 * (j % 2) - 1)) % N_Z
+
+    def chunk(slot, j):
+        return blocks.at[slot, :, pl.ds((z + N_Z - shift(j)) % N_Z * N_X, N_X)]
+
+    def turn(j, dx):
+        target = (z + shift(j)) % N_Z * N_X + (x + dx) % N_X
+        pltpu.make_async_remote_copy(
+            src_ref=spectra.at[target], dst_ref=blocks.at[bcol, :, freq], send_sem=turn_send, recv_sem=turn_recv.at[j],
+            device_id=(target, brow, bcol), device_id_type=MESH,
+        ).start()
+
+    def pass_on(source, target, peer, send, recv):
+        pltpu.make_async_remote_copy(
+            src_ref=source, dst_ref=target, send_sem=send, recv_sem=recv, device_id=peer, device_id_type=MESH
+        ).start()
+
+    def arrived(ref, semaphore):
+        pltpu.make_async_copy(ref, ref, semaphore).wait()
+
+    own = pltpu.make_async_copy(spectra.at[freq], blocks.at[bcol, :, freq], local)
+    own.start()
+    for dx in range(1, N_X):
+        turn(0, dx)
+
+    def send_row(j, carry):
+        for dx in range(N_X):
+            turn(j, dx)
+        return carry
+
+    lax.fori_loop(1, N_Z, send_row, 0)
+
+    def spread_own(j):
+        held = chunk(bcol, j)
+        pass_on(held, held, (freq, brow, near), near_send, near_recv.at[j])
+        pass_on(held, held, (freq, brow, other_core), core_send, core_recv)
+
+    def spread_near(j):
+        held = chunk(near, j)
+        arrived(held, near_recv.at[j])
+        pass_on(held, held, (freq, brow, other_core), relay_send, relay_recv)
+        pass_on(held, chunk(N_BCOL, j), (freq, 1 - brow, near), far_send, far_recv)
+
+    own.wait()
+    arrived(blocks.at[bcol, :, pl.ds(0, N_X - 1)], turn_recv.at[0])
+    spread_own(0)
+
+    def row(j, carry):
+        arrived(chunk(bcol, j), turn_recv.at[j])
+        spread_own(j)
+        spread_near(j - 1)
+        return carry
+
+    lax.fori_loop(1, N_Z, row, 0)
+    spread_near(N_Z - 1)
+    arrived(spectra.at[pl.ds(0, GROUPS - 1)], turn_send)
+    for semaphore in (near_send, core_send, relay_send, far_send, core_recv, relay_recv, far_recv):
+        arrived(blocks.at[0], semaphore)
+
+
 def exchange(spectra):
-    owned = lax.all_to_all(spectra.reshape(GROUPS, OWNED, ROWS, KEPT), "freq", split_axis=0, concat_axis=0, tiled=True)
-    owned = owned.transpose(1, 0, 2, 3).reshape(OWNED, 256, KEPT)
-    left = lax.all_gather(owned, "bcol", axis=0)
-    right = lax.all_gather(owned, "brow", axis=0)
-    other = lax.dynamic_index_in_dim(right, 1 - lax.axis_index("brow"), 0)
-    return jnp.concatenate([left, other], axis=0)
+    anywhere = pl.BlockSpec(memory_space=pl.ANY)
+    dma = pltpu.SemaphoreType.DMA
+    blocks = pl.pallas_call(
+        exchange_kernel,
+        out_shape=jax.ShapeDtypeStruct((N_BCOL + 1, OWNED, GROUPS, ROWS, KEPT), BF16),
+        in_specs=[anywhere],
+        out_specs=anywhere,
+        scratch_shapes=[dma, dma, dma((N_Z,)), dma, dma, dma, dma, dma((N_Z,)), dma, dma, dma],
+        compiler_params=pltpu.CompilerParams(collective_id=0, has_side_effects=True),
+        name="exchange",
+    )(spectra.reshape(GROUPS, OWNED, ROWS, KEPT))
+    return blocks.reshape(N_BCOL + 1, OWNED, GROUPS * ROWS, KEPT)
 
 
 def shards(voltages, fir_taps):

time: 118 us -> 48.2 us (0.41); the launches traced: 116 us -> 48 us
  waiting for transfers between devices: 56 us -> 0 us
  Pallas kernels: 12.2 us -> 47.4 us
  blocking collectives: 28.4 us -> 0 us
  between operations: 13.4 us -> 0.01 us
  other arithmetic: 3.93 us -> 0.59 us
  local copies, waits for them, and re-layouts: 1.9 us -> 0 us
    all_gather x2 -> x0, waiting for transfers between devices: 55.3 us -> none  [the longest x1 31.7 us: exchange(): left = lax.all_gather(owned, 'bcol', axis=0)]
    pallas_call x0 -> x1, Pallas kernels: none -> 35.2 us  [exchange(): pl.pallas_call(exchange_kernel, out_shape=jax.ShapeDtypeStruct((N_BCOL +...]
    all_to_all x1 -> x0, blocking collectives: 28.4 us -> none  [exchange(): lax.all_to_all(spectra.reshape(GROUPS, OWNED, ROWS, KEPT), 'freq', split_...]
    concatenate x1 -> x0, other arithmetic: 3.33 us -> none  [exchange(): return jnp.concatenate([left, other], axis=0)]
  transfers between devices with their start and end apart: 2 -> 0, of which waited for: 2 -> 0; matrix products, arithmetic and copies ran while one was open for 1% -> 0% of each run, Pallas kernels for 0% -> 0%
where the time goes in v2:
time: 48.2 us; the launch traced here: 48 us
  Pallas kernels  47.4 us (98%)
  other arithmetic  0.59 us (1%)
    pallas_call x1, Pallas kernels, exchange(): pl.pallas_call(exchange_kernel, out_shape=jax.ShapeDtypeStruct((N_BCOL +...  35.2 us
    pallas_call x1, Pallas kernels, correlate(): pl.pallas_call(correlate_kernel, grid_spec=grid_spec, out_shape=jax.Shape...  6.42 us
    pallas_call x1, Pallas kernels, channelize(): pl.pallas_call(channelize_kernel, out_shape=jax.ShapeDtypeStruct((GROUPS...  5.74 us

profile of v2, /device:TPU:2, one launch (start us, length us, event | category | flops | bytes accessed | tf_op | source)
XLA Modules:
  0.0 48.0 jit_solution(3353059383412410223)
XLA Ops:
  0.0 0.6 %pad_add_fusion.slots_ref = s32[2]{0:T(128)} fusion(s32[1]{0:T(128)} %bitcast.1, s32[1]{0:T(128)} %bitcast), kind=kLoop, calls=%fused_computation | loop fusion | flops 2 | bytes 16 | tf_op jit(solution)/shard_map/stack | solution.py:277
  0.6 5.7 %channelize.1 = bf16[1024,256]{1,0:T(8,128)(2,1)} custom-call(bf16[2,4,94208]{2,1,0:T(4,128)(2,1)} %x_ref.1, f32[16,4096]{1,0:T(8,128)} %taps_ref.1, bf16[2,256,256]{2,1,0:T(8,128)(2,1)} %constant.19.clone.first_ref, bf16[2,256,256]{2,1,0:T(8,128)(2,1)} %constant.20.clone.second_ref, f32[2,32,128]{2,1,0:T(8,128)} %constant.21.clone.turn_ref), custom_call_target="tpu_custom_call" | custom-call | tf_op jit(solution)/shard_map/channelize/pallas_call | solution.py:118
  6.3 35.2 %exchange.1 = bf16[5,4,32,8,256]{4,3,2,1,0:T(8,128)(2,1)} custom-call(bf16[32,4,8,256]{3,2,1,0:T(8,128)(2,1)} %bitcast.10), custom_call_target="tpu_custom_call" | custom-call | tf_op jit(solution)/shard_map/exchange/pallas_call | solution.py:261
  41.6 6.4 %correlate.1 = f32[2,4,1024,128]{3,2,1,0:T(8,128)} custom-call(s32[2]{0:T(128)} %pad_add_fusion.slots_ref, bf16[5,4,256,256]{3,2,1,0:T(8,128)(2,1)} %bitcast.7, bf16[5,4,256,256]{3,2,1,0:T(8,128)(2,1)} %bitcast.8, bf16[5,4,256,256]{3,2,1,0:T(8,128)(2,1)} %bitcast.9, bf16[256,256]{1,0:T(8,128)(2,1)} %constant.22.clone.sort_ref), custom_call_target="tpu_custom_call" | custom-call | tf_op jit(solution)/shard_map/correlate/pallas_call | solution.py:168

commit v3 on v2

v3 whole, which is shorter than its diff:
```python
import functools
import math

import jax
import jax.numpy as jnp
import numpy as np
from jax import lax
from jax.experimental import pallas as pl
from jax.experimental.pallas import tpu as pltpu
from jax.sharding import PartitionSpec as P

CHANNELS = 4096
SCALE = 1.0 / 64.0
TAPS = 16
AVG = 32
FRAMES = 8
SLOW = 32
FAST = 128
WIDTH = 4
OWNED = 4
GROUPS = 32
KEPT = FRAMES * SLOW
ROWS = 2 * WIDTH
N_X = 4
N_Z = 8
N_BCOL = 4
MESH = pl.DeviceIdType.MESH
F32 = jnp.float32
BF16 = jnp.bfloat16


def halves(table):
    high = table.astype(np.float32).astype(jnp.bfloat16)
    low = (table - high.astype(np.float64)).astype(np.float32).astype(jnp.bfloat16)
    return high, low


def tables():
    b, k1 = np.arange(SLOW), np.arange(SLOW)
    angle = 2.0 * np.pi * (np.outer(k1, b) % SLOW) / SLOW
    first = np.zeros((2, WIDTH, SLOW, SLOW, 2, WIDTH))
    for s in range(WIDTH):
        first[0, s, :, :, 0, s] = np.cos(angle)
        first[0, s, :, :, 1, s] = np.sin(angle)
        first[1, s, :, :, 0, s] = -np.sin(angle)
        first[1, s, :, :, 1, s] = np.cos(angle)
    first = first.reshape(256, 256)
    n, m = np.arange(FAST), np.arange(FAST)
    angle = 2.0 * np.pi * (np.outer(m, n) % FAST) / FAST
    second = np.zeros((FAST, 2, 2, FAST))
    second[:, 0, 0, :] = np.cos(angle)
    second[:, 0, 1, :] = np.sin(angle)
    second[:, 1, 0, :] = -np.sin(angle)
    second[:, 1, 1, :] = np.cos(angle)
    second = second.reshape(256, 256) * SCALE
    angle = 2.0 * np.pi * np.outer(k1, n) / CHANNELS
    turn = np.stack([np.cos(angle), np.sin(angle)]).astype(np.float32)
    sort = np.zeros((2, GROUPS, WIDTH, GROUPS, 2, WIDTH), np.float32)
    for d in range(2):
        for g in range(GROUPS):
            for s in range(WIDTH):
                sort[d, g, s, g, d, s] = 1.0
    sort = sort.reshape(256, 256).astype(jnp.bfloat16)
    return np.stack(halves(first)), np.stack(halves(second)), turn, sort


FIRST, SECOND, TURN, SORT = tables()
NT = (((1,), (1,)), ((), ()))


def split(value):
    high = value.astype(BF16)
    low = (value - high.astype(F32)).astype(BF16)
    return high, low


def channelize(load, taps_ref, first_ref, second_ref, turn_ref, spectra, fir, spread):
    def column(b, carry):
        lanes = pl.multiple_of(b * FAST, FAST)
        rows = pl.multiple_of(b * ROWS, ROWS)
        frames = []
        for j in range(FRAMES + TAPS - 1):
            real, imag = load(pl.multiple_of(j * CHANNELS + lanes, FAST))
            frames.append(jnp.concatenate([real.astype(F32), imag.astype(F32)], axis=0))
        taps = [taps_ref[pl.ds(p, 1), pl.ds(lanes, FAST)] for p in range(TAPS)]
        for t in range(FRAMES):
            total = taps[0] * frames[t]
            for p in range(1, TAPS):
                total = total + taps[p] * frames[t + p]
            fir[pl.ds(rows, ROWS), t * FAST:(t + 1) * FAST] = total
        return carry

    lax.fori_loop(0, SLOW, column, 0, unroll=4)
    high, low = split(fir[...])
    dot = functools.partial(jnp.dot, preferred_element_type=F32)
    section = dot(first_ref[0], high) + dot(first_ref[1], high) + dot(first_ref[0], low)
    cosine, sine = turn_ref[0], turn_ref[1]
    for s in range(WIDTH):
        parts = []
        for t in range(FRAMES):
            real = section[s * SLOW:(s + 1) * SLOW, t * FAST:(t + 1) * FAST]
            imag = section[128 + s * SLOW:128 + (s + 1) * SLOW, t * FAST:(t + 1) * FAST]
            parts.append(jnp.concatenate([real * cosine + imag * sine, imag * cosine - real * sine], axis=1))
        high, low = split(jnp.concatenate(parts, axis=0))
        dot_nt = functools.partial(lax.dot_general, dimension_numbers=NT, preferred_element_type=F32)
        spectrum = dot_nt(second_ref[0], high) + dot_nt(second_ref[1], high) + dot_nt(second_ref[0], low)
        for half in range(2):
            lanes = slice(half * 128, (half + 1) * 128)
            spread[half, pl.ds(s, 256, stride=WIDTH), :] = spectrum[:, lanes]
    for half in range(2):
        lanes = slice(half * 128, (half + 1) * 128)
        spectra[:, :, :, lanes] = spread[half].reshape(GROUPS, OWNED, ROWS, 128).astype(BF16)


SCHEDULE = tuple((k[0], int(k[1])) for k in ("o0", "o1", "n0", "o2", "o3", "n1", "o4", "o5", "n2", "o6", "n3", "o7", "n4", "n5", "n6", "n7"))


def spectra_kernel(
    x_hbm, taps_hbm, first_hbm, second_hbm, turn_hbm, blocks, x_ref, taps_ref, first_ref, second_ref, turn_ref, fir, spread,
    spectra, load_sem, local, turn_send, turn_recv, near_send, core_send, relay_send, far_send, near_recv, core_recv,
    relay_recv, far_recv
):
    loads = [
        pltpu.make_async_copy(source, target, load_sem.at[i])
        for i, (source, target) in enumerate(
            ((x_hbm, x_ref), (taps_hbm, taps_ref), (first_hbm, first_ref), (second_hbm, second_ref), (turn_hbm, turn_ref))
        )
    ]
    for copy in loads:
        copy.start()

    freq, brow, bcol = lax.axis_index("freq"), lax.axis_index("brow"), lax.axis_index("bcol")
    z, x = freq // N_X, freq % N_X
    y_low, core = bcol // 2, bcol % 2
    other_core = 2 * y_low + 1 - core
    near = 2 * (1 - y_low) + core

    barrier = pltpu.get_barrier_semaphore()

    def greet(i, carry):
        pl.semaphore_signal(barrier, inc=1, device_id=((freq + i) % GROUPS, brow, bcol), device_id_type=MESH)
        return carry

    lax.fori_loop(1, GROUPS, greet, 0)
    for peer in ((freq, brow, other_core), (freq, brow, near), (freq, 1 - brow, near)):
        pl.semaphore_signal(barrier, inc=1, device_id=peer, device_id_type=MESH)

    for copy in loads:
        copy.wait()

    def load(at):
        return x_ref[0, :, pl.ds(at, FAST)], x_ref[1, :, pl.ds(at, FAST)]

    channelize(load, taps_ref, first_ref, second_ref, turn_ref, spectra, fir, spread)
    pl.semaphore_wait(barrier, GROUPS - 1 + 3)

    def shift(j):
        return (N_Z + ((j + 1) // 2) * (2 * (j % 2) - 1)) % N_Z

    def chunk(slot, j):
        return blocks.at[slot, :, pl.ds((z + N_Z - shift(j)) % N_Z * N_X, N_X)]

    def turn(j, dx):
        target = (z + shift(j)) % N_Z * N_X + (x + dx) % N_X
        pltpu.make_async_remote_copy(
            src_ref=spectra.at[target], dst_ref=blocks.at[bcol, :, freq], send_sem=turn_send, recv_sem=turn_recv.at[j],
            device_id=(target, brow, bcol), device_id_type=MESH,
        ).start()

    def pass_on(source, target, peer, send, recv):
        pltpu.make_async_remote_copy(
            src_ref=source, dst_ref=target, send_sem=send, recv_sem=recv, device_id=peer, device_id_type=MESH
        ).start()

    def arrived(ref, semaphore):
        pltpu.make_async_copy(ref, ref, semaphore).wait()

    own = pltpu.make_async_copy(spectra.at[freq], blocks.at[bcol, :, freq], local)
    own.start()
    for dx in range(1, N_X):
        turn(0, dx)

    def send_row(j, carry):
        for dx in range(N_X):
            turn(j, dx)
        return carry

    lax.fori_loop(1, N_Z, send_row, 0)

    def spread_own(j):
        if j == 0:
            own.wait()
            arrived(blocks.at[bcol, :, pl.ds(0, N_X - 1)], turn_recv.at[0])
        else:
            arrived(chunk(bcol, j), turn_recv.at[j])
        held = chunk(bcol, j)
        pass_on(held, held, (freq, brow, near), near_send, near_recv.at[j])
        pass_on(held, held, (freq, brow, other_core), core_send, core_recv)

    def spread_near(j):
        held = chunk(near, j)
        arrived(held, near_recv.at[j])
        pass_on(held, chunk(N_BCOL, j), (freq, 1 - brow, near), far_send, far_recv)
        pass_on(held, held, (freq, brow, other_core), relay_send, relay_recv)

    for kind, j in SCHEDULE:
        (spread_own if kind == "o" else spread_near)(j)
    arrived(spectra.at[pl.ds(0, GROUPS - 1)], turn_send)
    for semaphore in (near_send, core_send, relay_send, far_send, core_recv, relay_recv, far_recv):
        arrived(blocks.at[0], semaphore)


def spread_spectra(voltages, fir_taps):
    anywhere = pl.BlockSpec(memory_space=pl.ANY)
    dma = pltpu.SemaphoreType.DMA
    blocks = pl.pallas_call(
        spectra_kernel,
        out_shape=jax.ShapeDtypeStruct((N_BCOL + 1, OWNED, GROUPS, ROWS, KEPT), BF16),
        in_specs=[pl.BlockSpec(memory_space=pltpu.HBM)] * 5,
        out_specs=anywhere,
        scratch_shapes=[
            pltpu.VMEM(voltages.shape, BF16),
            pltpu.VMEM(fir_taps.shape, F32),
            pltpu.VMEM(FIRST.shape, BF16),
            pltpu.VMEM(SECOND.shape, BF16),
            pltpu.VMEM(TURN.shape, F32),
            pltpu.VMEM((256, FRAMES * FAST), F32),
            pltpu.VMEM((2, GROUPS * OWNED * ROWS, 128), F32),
            pltpu.VMEM((GROUPS, OWNED, ROWS, KEPT), BF16),
            dma((5,)), dma, dma, dma((N_Z,)), dma, dma, dma, dma, dma((N_Z,)), dma, dma, dma,
        ],
        compiler_params=pltpu.CompilerParams(collective_id=0, has_side_effects=True, vmem_limit_bytes=24 * 2**20),
        name="spectra",
    )(*[pltpu.with_memory_space_constraint(v, pltpu.HBM) for v in (voltages, fir_taps, jnp.asarray(FIRST), jnp.asarray(SECOND), jnp.asarray(TURN))])
    return blocks.reshape(N_BCOL + 1, OWNED, GROUPS * ROWS, KEPT)


def correlate_kernel(held, sort_ref, out, built, store_sem):
    brow, bcol = lax.axis_index("brow"), lax.axis_index("bcol")
    slots = (bcol + brow * (N_BCOL - bcol), N_BCOL - brow * (N_BCOL - bcol))
    upper = lax.broadcasted_iota(jnp.int32, (GROUPS, ROWS, 256), 1) < WIDTH
    stores = []
    for q in range(OWNED):
        sort = sort_ref[...]
        parts = [jnp.dot(sort, held[slot, q], preferred_element_type=F32).astype(BF16) for slot in slots]
        right = jnp.concatenate([parts[0][:128], parts[1][:128], parts[0][128:], parts[1][128:]], axis=0)
        for block in range(N_BCOL):
            product = lax.dot_general(held[block, q], right, NT, preferred_element_type=F32)
            with_real = product[:, :256].reshape(GROUPS, ROWS, 256)
            with_imag = pltpu.roll(product[:, 256:].reshape(GROUPS, ROWS, 256), WIDTH, axis=1)
            mixed = (with_real + jnp.where(upper, with_imag, -with_imag)) * (1.0 / (FRAMES * AVG))
            pairs = mixed.reshape(GROUPS // 2, 2, ROWS, 256)
            even, odd = pairs[:, 0], pairs[:, 1]
            real = jnp.where(upper[:GROUPS // 2], even, pltpu.roll(odd, WIDTH, axis=1)).reshape(128, 256)
            imag = jnp.where(upper[:GROUPS // 2], pltpu.roll(even, WIDTH, axis=1), odd).reshape(128, 256)
            for r in range(2):
                rows = pl.ds(block * 256 + r, 128, stride=2)
                built[0, q, rows, :] = real[:, r * 128:(r + 1) * 128]
                built[1, q, rows, :] = imag[:, r * 128:(r + 1) * 128]
            part = (slice(None), q, pl.ds(block * 256, 256))
            stores.append(pltpu.make_async_copy(built.at[part], out.at[part], store_sem.at[q, block]))
            stores[-1].start()
    for copy in stores:
        copy.wait()


def correlate(blocks):
    vmem = pl.BlockSpec(memory_space=pltpu.VMEM)
    shape = (2, OWNED, 1024, 128)
    return pl.pallas_call(
        correlate_kernel,
        out_shape=jax.ShapeDtypeStruct(shape, F32),
        in_specs=[vmem] * 2,
        out_specs=pl.BlockSpec(memory_space=pltpu.HBM),
        scratch_shapes=[pltpu.VMEM(shape, F32), pltpu.SemaphoreType.DMA((OWNED, N_BCOL))],
        compiler_params=pltpu.CompilerParams(vmem_limit_bytes=24 * 2**20),
        name="correlate",
    )(blocks, jnp.asarray(SORT))


def shards(voltages, fir_taps):
    blocks = spread_spectra(voltages, fir_taps)
    return correlate(blocks).reshape(2, OWNED, 512, 2, 1, 128)


def solution(mesh):
    in_specs = (P(None, ("brow", "bcol", "freq"), None), P())
    out_specs = P(None, "freq", "brow", None, "bcol", None)
    return jax.shard_map(shards, mesh=mesh, in_specs=in_specs, out_specs=out_specs, check_vma=False)
```

time: 48.2 us -> 36.6 us (0.76)
  Pallas kernels: 47.4 us -> 36.5 us
  other arithmetic: 0.59 us -> 0 us
    pallas_call x3 -> x2, Pallas kernels: 47.4 us -> 36.5 us  [the longest x1 33.5 us: spread_spectra(): pl.pallas_call(spectra_kernel, out_shape=jax.ShapeDtypeStruct((N_BCOL + 1...]
    another operation x1 -> x0, other arithmetic: 0.59 us -> none  [shards(): jnp.stack([bcol + brow * (4 - bcol), 4 - brow * (4 - bcol)])]
where the time goes in v3:
time: 36.6 us; the launch traced here: 36.5 us
  Pallas kernels  36.5 us (100%)
    pallas_call x1, Pallas kernels, spread_spectra(): pl.pallas_call(spectra_kernel, out_shape=jax.ShapeDtypeStruct((N_BCOL + 1...  33.5 us
    pallas_call x1, Pallas kernels, correlate(): pl.pallas_call(correlate_kernel, out_shape=jax.ShapeDtypeStruct(shape, F3...  2.98 us

profile of v3, /device:TPU:2, one launch (start us, length us, event | category | flops | bytes accessed | tf_op | source)
XLA Modules:
  0.0 36.5 jit_solution(13847103022790238791)
XLA Ops:
  0.0 0.0 copy-start
  0.0 33.5 %spectra.1 = bf16[5,4,32,8,256]{4,3,2,1,0:T(8,128)(2,1)S(1)} custom-call(bf16[2,4,94208]{2,1,0:T(4,128)(2,1)} %x_hbm.1, f32[16,4096]{1,0:T(8,128)} %taps_hbm.1, bf16[2,256,256]{2,1,0:T(8,128)(2,1)} %constant.8.clone.first_hbm, bf16[2,256,256]{2,1,0:T(8,128)(2,1)} %constant.9.clone.second_hbm, f32[2,32,128]{2,1,0:T(8,128)} %constant.10.clone.turn_hbm), custom_call_target="tpu_custom_call" | custom-call | tf_op jit(solution)/shard_map/spectra/pallas_call | solution.py:216
  33.5 0.0 copy-done
  33.5 3.0 %correlate.1 = f32[2,4,1024,128]{3,2,1,0:T(8,128)} custom-call(bf16[5,4,256,256]{3,2,1,0:T(8,128)(2,1)S(1)} %bitcast.4, bf16[256,256]{1,0:T(8,128)(2,1)S(1)} %copy-done), custom_call_target="tpu_custom_call" | custom-call | tf_op jit(solution)/shard_map/correlate/pallas_call | solution.py:270
Async XLA Ops:
  0.0 33.5 %copy-start = (bf16[256,256]{1,0:T(8,128)(2,1)S(1)}, bf16[256,256]{1,0:T(8,128)(2,1)}, u32[]{:S(2)}) copy-start(bf16[256,256]{1,0:T(8,128)(2,1)} %constant.11.clone.sort_ref) | copy-start | bytes 393220

commit v4 on v3

--- a/solution.py
+++ b/solution.py
@@ -19,6 +19,9 @@
 WIDTH = 4
 OWNED = 4
 GROUPS = 32
+N_SHIFTS = GROUPS - 1
+LOADS = 2
+SPAN = CHANNELS // LOADS
 KEPT = FRAMES * SLOW
 ROWS = 2 * WIDTH
 N_X = 4
@@ -74,14 +77,14 @@
     return high, low
 
 
-def channelize(load, taps_ref, first_ref, second_ref, turn_ref, spectra, fir, spread):
-    def column(b, carry):
-        lanes = pl.multiple_of(b * FAST, FAST)
-        rows = pl.multiple_of(b * ROWS, ROWS)
+def channelize(x_ref, ready, tables_ready, taps_ref, first_ref, second_ref, turn_ref, spectra, fir, spread):
+    def column(group, b, carry):
+        lanes = pl.multiple_of(group * SPAN + b * FAST, FAST)
+        rows = pl.multiple_of((group * (SPAN // FAST) + b) * ROWS, ROWS)
         frames = []
         for j in range(FRAMES + TAPS - 1):
-            real, imag = load(pl.multiple_of(j * CHANNELS + lanes, FAST))
-            frames.append(jnp.concatenate([real.astype(F32), imag.astype(F32)], axis=0))
+            at = pl.ds(pl.multiple_of(j * SPAN + b * FAST, FAST), FAST)
+            frames.append(jnp.concatenate([x_ref[group, c, :, at].astype(F32) for c in range(2)], axis=0))
         taps = [taps_ref[pl.ds(p, 1), pl.ds(lanes, FAST)] for p in range(TAPS)]
         for t in range(FRAMES):
             total = taps[0] * frames[t]
@@ -90,7 +93,10 @@
             fir[pl.ds(rows, ROWS), t * FAST:(t + 1) * FAST] = total
         return carry
 
-    lax.fori_loop(0, SLOW, column, 0, unroll=4)
+    for group in range(LOADS):
+        ready(group)
+        lax.fori_loop(0, SPAN // FAST, functools.partial(column, group), 0, unroll=4)
+    tables_ready()
     high, low = split(fir[...])
     dot = functools.partial(jnp.dot, preferred_element_type=F32)
     section = dot(first_ref[0], high) + dot(first_ref[1], high) + dot(first_ref[0], low)
@@ -112,21 +118,33 @@
         spectra[:, :, :, lanes] = spread[half].reshape(GROUPS, OWNED, ROWS, 128).astype(BF16)
 
 
-SCHEDULE = tuple((k[0], int(k[1])) for k in ("o0", "o1", "n0", "o2", "o3", "n1", "o4", "o5", "n2", "o6", "n3", "o7", "n4", "n5", "n6", "n7"))
+SHIFTS = ((0, 1), (0, 3), (1, 0), (7, 0), (4, 2), (0, 2), (1, 1), (1, 3), (2, 0), (6, 0), (7, 1), (7, 3), (3, 2), (4, 1), (4, 3), (5, 2), (1, 2), (2, 1), (2, 3), (3, 0), (5, 0), (6, 1), (6, 3), (7, 2), (2, 2), (3, 1), (3, 3), (4, 0), (5, 1), (5, 3), (6, 2))
+SCHEDULE = (('o', 0), ('o', 1), ('o', 2), ('n', 0), ('o', 3), ('n', 1), ('n', 5), ('o', 5), ('o', 6), ('o', 7), ('n', 2), ('o', 8), ('n', 3), ('o', 9), ('o', 10), ('o', 11), ('o', 4), ('n', 6), ('n', 7), ('n', 8), ('n', 9), ('o', 16), ('o', 12), ('n', 10), ('o', 17), ('o', 13), ('n', 11), ('o', 18), ('o', 14), ('n', 4), ('o', 19), ('o', 15), ('o', 20), ('o', 21), ('o', 22), ('o', 23), ('n', 16), ('n', 12), ('o', 24), ('n', 17), ('o', 25), ('n', 13), ('o', 26), ('n', 18), ('o', 27), ('n', 14), ('o', 28), ('n', 19), ('o', 29), ('n', 15), ('o', 30), ('n', 20), ('n', 21), ('n', 22), ('n', 23), ('n', 24), ('n', 25), ('n', 26), ('n', 27), ('n', 28), ('n', 29), ('n', 30))
 
 
 def spectra_kernel(
     x_hbm, taps_hbm, first_hbm, second_hbm, turn_hbm, blocks, x_ref, taps_ref, first_ref, second_ref, turn_ref, fir, spread,
-    spectra, load_sem, local, turn_send, turn_recv, near_send, core_send, relay_send, far_send, near_recv, core_recv,
+    spectra, load_sem, frame_sem, local, turn_send, turn_recv, near_send, core_send, relay_send, far_send, near_recv, core_recv,
     relay_recv, far_recv
 ):
     loads = [
         pltpu.make_async_copy(source, target, load_sem.at[i])
         for i, (source, target) in enumerate(
-            ((x_hbm, x_ref), (taps_hbm, taps_ref), (first_hbm, first_ref), (second_hbm, second_ref), (turn_hbm, turn_ref))
+            ((taps_hbm, taps_ref), (first_hbm, first_ref), (second_hbm, second_ref), (turn_hbm, turn_ref))
         )
     ]
-    for copy in loads:
+    loads[0].start()
+
+    def load_frames(group):
+        for j in range(FRAMES + TAPS - 1):
+            pltpu.make_async_copy(
+                x_hbm.at[:, :, pl.ds(j * CHANNELS + group * SPAN, SPAN)], x_ref.at[group, :, :, pl.ds(j * SPAN, SPAN)],
+                frame_sem.at[group],
+            ).start()
+
+    for group in range(LOADS):
+        load_frames(group)
+    for copy in loads[1:]:
         copy.start()
 
     freq, brow, bcol = lax.axis_index("freq"), lax.axis_index("brow"), lax.axis_index("bcol")
@@ -145,31 +163,31 @@
     for peer in ((freq, brow, other_core), (freq, brow, near), (freq, 1 - brow, near)):
         pl.semaphore_signal(barrier, inc=1, device_id=peer, device_id_type=MESH)
 
-    for copy in loads:
-        copy.wait()
-
-    def load(at):
-        return x_ref[0, :, pl.ds(at, FAST)], x_ref[1, :, pl.ds(at, FAST)]
-
-    channelize(load, taps_ref, first_ref, second_ref, turn_ref, spectra, fir, spread)
-    pl.semaphore_wait(barrier, GROUPS - 1 + 3)
-
-    def shift(j):
-        return (N_Z + ((j + 1) // 2) * (2 * (j % 2) - 1)) % N_Z
-
-    def chunk(slot, j):
-        return blocks.at[slot, :, pl.ds((z + N_Z - shift(j)) % N_Z * N_X, N_X)]
-
-    def turn(j, dx):
-        target = (z + shift(j)) % N_Z * N_X + (x + dx) % N_X
+    for dx in range(1, N_X):
+        peer = (z * N_X + (x + dx) % N_X, brow, near)
+        pl.semaphore_signal(barrier, inc=1, device_id=peer, device_id_type=MESH)
+
+    loads[0].wait()
+
+    def ready(group):
+        pltpu.make_async_copy(x_ref.at[group], x_ref.at[group], frame_sem.at[group]).wait()
+
+    def tables_ready():
+        for copy in loads[1:]:
+            copy.wait()
+
+    channelize(x_ref, ready, tables_ready, taps_ref, first_ref, second_ref, turn_ref, spectra, fir, spread)
+    pl.semaphore_wait(barrier, GROUPS - 1 + 3 + N_X - 1)
+
+    def group_of(dz, dx):
+        return (z + N_Z - dz) % N_Z * N_X + (x + N_X - dx) % N_X
+
+    def row_of(slot, dz):
+        return blocks.at[slot, :, pl.ds((z + N_Z - dz) % N_Z * N_X, N_X)]
+
+    def send(source, target, peer, send_sem, recv_sem):
         pltpu.make_async_remote_copy(
-            src_ref=spectra.at[target], dst_ref=blocks.at[bcol, :, freq], send_sem=turn_send, recv_sem=turn_recv.at[j],
-            device_id=(target, brow, bcol), device_id_type=MESH,
-        ).start()
-
-    def pass_on(source, target, peer, send, recv):
-        pltpu.make_async_remote_copy(
-            src_ref=source, dst_ref=target, send_sem=send, recv_sem=recv, device_id=peer, device_id_type=MESH
+            src_ref=source, dst_ref=target, send_sem=send_sem, recv_sem=recv_sem, device_id=peer, device_id_type=MESH
         ).start()
 
     def arrived(ref, semaphore):
@@ -177,34 +195,41 @@
 
     own = pltpu.make_async_copy(spectra.at[freq], blocks.at[bcol, :, freq], local)
     own.start()
-    for dx in range(1, N_X):
-        turn(0, dx)
-
-    def send_row(j, carry):
-        for dx in range(N_X):
-            turn(j, dx)
-        return carry
-
-    lax.fori_loop(1, N_Z, send_row, 0)
-
-    def spread_own(j):
-        if j == 0:
-            own.wait()
-            arrived(blocks.at[bcol, :, pl.ds(0, N_X - 1)], turn_recv.at[0])
-        else:
-            arrived(chunk(bcol, j), turn_recv.at[j])
-        held = chunk(bcol, j)
-        pass_on(held, held, (freq, brow, near), near_send, near_recv.at[j])
-        pass_on(held, held, (freq, brow, other_core), core_send, core_recv)
-
-    def spread_near(j):
-        held = chunk(near, j)
-        arrived(held, near_recv.at[j])
-        pass_on(held, chunk(N_BCOL, j), (freq, 1 - brow, near), far_send, far_recv)
-        pass_on(held, held, (freq, brow, other_core), relay_send, relay_recv)
-
-    for kind, j in SCHEDULE:
-        (spread_own if kind == "o" else spread_near)(j)
+    send(spectra.at[freq], blocks.at[bcol, :, freq], (freq, brow, near), near_send, near_recv.at[N_SHIFTS])
+    for i, (dz, dx) in enumerate(SHIFTS):
+        target = group_of(N_Z - dz, N_X - dx)
+        send(spectra.at[target], blocks.at[bcol, :, freq], (target, brow, bcol), turn_send, turn_recv.at[i])
+        if dz == 0:
+            send(spectra.at[target], blocks.at[bcol, :, freq], (target, brow, near), near_send, near_recv.at[i])
+    own.wait()
+    held_own, held_near = [N_X] * N_Z, [N_X] * N_Z
+    held_own[0] -= 1
+
+    def take_own(i):
+        dz, dx = SHIFTS[i]
+        held = blocks.at[bcol, :, group_of(dz, dx)]
+        arrived(held, turn_recv.at[i])
+        if dz:
+            send(held, held, (freq, brow, near), near_send, near_recv.at[i])
+        held_own[dz] -= 1
+        if not held_own[dz]:
+            row = row_of(bcol, dz)
+            send(row, row, (freq, brow, other_core), core_send, core_recv)
+
+    def take_near(i):
+        dz, dx = SHIFTS[i] if i < N_SHIFTS else (0, 0)
+        group = group_of(dz, dx)
+        held = blocks.at[near, :, group]
+        arrived(held, near_recv.at[i])
+        send(held, blocks.at[N_BCOL, :, group], (freq, 1 - brow, near), far_send, far_recv)
+        held_near[dz] -= 1
+        if not held_near[dz]:
+            row = row_of(near, dz)
+            send(row, row, (freq, brow, other_core), relay_send, relay_recv)
+
+    take_near(N_SHIFTS)
+    for kind, i in SCHEDULE:
+        (take_own if kind == "o" else take_near)(i)
     arrived(spectra.at[pl.ds(0, GROUPS - 1)], turn_send)
     for semaphore in (near_send, core_send, relay_send, far_send, core_recv, relay_recv, far_recv):
         arrived(blocks.at[0], semaphore)
@@ -219,7 +244,7 @@
         in_specs=[pl.BlockSpec(memory_space=pltpu.HBM)] * 5,
         out_specs=anywhere,
         scratch_shapes=[
-            pltpu.VMEM(voltages.shape, BF16),
+            pltpu.VMEM((LOADS, 2, WIDTH, (FRAMES + TAPS - 1) * SPAN), BF16),
             pltpu.VMEM(fir_taps.shape, F32),
             pltpu.VMEM(FIRST.shape, BF16),
             pltpu.VMEM(SECOND.shape, BF16),
@@ -227,7 +252,7 @@
             pltpu.VMEM((256, FRAMES * FAST), F32),
             pltpu.VMEM((2, GROUPS * OWNED * ROWS, 128), F32),
             pltpu.VMEM((GROUPS, OWNED, ROWS, KEPT), BF16),
-            dma((5,)), dma, dma, dma((N_Z,)), dma, dma, dma, dma, dma((N_Z,)), dma, dma, dma,
+            dma((4,)), dma((LOADS,)), dma, dma, dma((N_SHIFTS,)), dma, dma, dma, dma, dma((N_SHIFTS + 1,)), dma, dma, dma,
         ],
         compiler_params=pltpu.CompilerParams(collective_id=0, has_side_effects=True, vmem_limit_bytes=24 * 2**20),
         name="spectra",

time: 36.6 us -> 35.7 us (0.975)
  Pallas kernels: 36.5 us -> 35.5 us
    pallas_call x1, Pallas kernels: 33.5 us -> 32.6 us  [spread_spectra(): pl.pallas_call(spectra_kernel, out_shape=jax.ShapeDtypeStruct((N_BCOL + 1...]
where the time goes in v4:
time: 35.7 us; the launch traced here: 35.6 us
  Pallas kernels  35.5 us (99%)
    pallas_call x1, Pallas kernels, spread_spectra(): pl.pallas_call(spectra_kernel, out_shape=jax.ShapeDtypeStruct((N_BCOL + 1...  32.6 us
    pallas_call x1, Pallas kernels, correlate(): pl.pallas_call(correlate_kernel, out_shape=jax.ShapeDtypeStruct(shape, F3...  2.98 us

profile of v4, /device:TPU:2, one launch (start us, length us, event | category | flops | bytes accessed | tf_op | source)
XLA Modules:
  0.0 35.6 jit_solution(14477195597948764721)
XLA Ops:
  0.0 0.0 copy-start
  0.0 32.6 %spectra.1 = bf16[5,4,32,8,256]{4,3,2,1,0:T(8,128)(2,1)S(1)} custom-call(bf16[2,4,94208]{2,1,0:T(4,128)(2,1)} %x_hbm.1, f32[16,4096]{1,0:T(8,128)} %taps_hbm.1, bf16[2,256,256]{2,1,0:T(8,128)(2,1)} %constant.8.clone.first_hbm, bf16[2,256,256]{2,1,0:T(8,128)(2,1)} %constant.9.clone.second_hbm, f32[2,32,128]{2,1,0:T(8,128)} %constant.10.clone.turn_hbm), custom_call_target="tpu_custom_call" | custom-call | tf_op jit(solution)/shard_map/spectra/pallas_call | solution.py:241
  32.6 0.0 copy-done
  32.6 3.0 %correlate.1 = f32[2,4,1024,128]{3,2,1,0:T(8,128)} custom-call(bf16[5,4,256,256]{3,2,1,0:T(8,128)(2,1)S(1)} %bitcast.4, bf16[256,256]{1,0:T(8,128)(2,1)S(1)} %copy-done), custom_call_target="tpu_custom_call" | custom-call | tf_op jit(solution)/shard_map/correlate/pallas_call | solution.py:295
Async XLA Ops:
  0.0 32.6 %copy-start = (bf16[256,256]{1,0:T(8,128)(2,1)S(1)}, bf16[256,256]{1,0:T(8,128)(2,1)}, u32[]{:S(2)}) copy-start(bf16[256,256]{1,0:T(8,128)(2,1)} %constant.11.clone.sort_ref) | copy-start | bytes 393220

commit v5 on v4

--- a/solution.py
+++ b/solution.py
@@ -118,8 +118,8 @@
         spectra[:, :, :, lanes] = spread[half].reshape(GROUPS, OWNED, ROWS, 128).astype(BF16)
 
 
-SHIFTS = ((0, 1), (0, 3), (1, 0), (7, 0), (4, 2), (0, 2), (1, 1), (1, 3), (2, 0), (6, 0), (7, 1), (7, 3), (3, 2), (4, 1), (4, 3), (5, 2), (1, 2), (2, 1), (2, 3), (3, 0), (5, 0), (6, 1), (6, 3), (7, 2), (2, 2), (3, 1), (3, 3), (4, 0), (5, 1), (5, 3), (6, 2))
-SCHEDULE = (('o', 0), ('o', 1), ('o', 2), ('n', 0), ('o', 3), ('n', 1), ('n', 5), ('o', 5), ('o', 6), ('o', 7), ('n', 2), ('o', 8), ('n', 3), ('o', 9), ('o', 10), ('o', 11), ('o', 4), ('n', 6), ('n', 7), ('n', 8), ('n', 9), ('o', 16), ('o', 12), ('n', 10), ('o', 17), ('o', 13), ('n', 11), ('o', 18), ('o', 14), ('n', 4), ('o', 19), ('o', 15), ('o', 20), ('o', 21), ('o', 22), ('o', 23), ('n', 16), ('n', 12), ('o', 24), ('n', 17), ('o', 25), ('n', 13), ('o', 26), ('n', 18), ('o', 27), ('n', 14), ('o', 28), ('n', 19), ('o', 29), ('n', 15), ('o', 30), ('n', 20), ('n', 21), ('n', 22), ('n', 23), ('n', 24), ('n', 25), ('n', 26), ('n', 27), ('n', 28), ('n', 29), ('n', 30))
+SHIFTS = ((0, 1), (0, 3), (1, 0), (7, 0), (0, 2), (1, 1), (1, 3), (2, 0), (6, 0), (7, 1), (7, 3), (4, 2), (3, 2), (4, 1), (4, 3), (5, 2), (1, 2), (2, 1), (2, 3), (3, 0), (5, 0), (6, 1), (6, 3), (7, 2), (2, 2), (3, 1), (3, 3), (4, 0), (5, 1), (5, 3), (6, 2))
+SCHEDULE = (('o', 0), ('o', 1), ('o', 2), ('n', 0), ('o', 3), ('n', 1), ('n', 4), ('o', 4), ('o', 5), ('o', 6), ('o', 7), ('n', 2), ('o', 8), ('n', 3), ('o', 9), ('o', 10), ('n', 5), ('n', 6), ('n', 7), ('n', 8), ('n', 9), ('o', 16), ('o', 12), ('n', 10), ('o', 17), ('o', 13), ('o', 11), ('o', 18), ('o', 14), ('o', 19), ('o', 15), ('o', 20), ('o', 21), ('o', 22), ('o', 23), ('n', 16), ('n', 12), ('o', 24), ('n', 17), ('o', 25), ('n', 13), ('o', 26), ('n', 11), ('o', 27), ('n', 18), ('o', 28), ('n', 14), ('o', 29), ('n', 19), ('o', 30), ('n', 15), ('n', 20), ('n', 21), ('n', 22), ('n', 23), ('n', 24), ('n', 25), ('n', 26), ('n', 27), ('n', 28), ('n', 29), ('n', 30))
 
 
 def spectra_kernel(

time: 35.7 us -> 35.4 us (level)
  no operation moved by 1% of the time
where the time goes in v5:
time: 35.4 us; the launch traced here: 35.3 us
  Pallas kernels  35.3 us (100%)
    pallas_call x1, Pallas kernels, spread_spectra(): pl.pallas_call(spectra_kernel, out_shape=jax.ShapeDtypeStruct((N_BCOL + 1...  32.3 us
    pallas_call x1, Pallas kernels, correlate(): pl.pallas_call(correlate_kernel, out_shape=jax.ShapeDtypeStruct(shape, F3...  2.99 us

profile of v5, /device:TPU:2, one launch (start us, length us, event | category | flops | bytes accessed | tf_op | source)
XLA Modules:
  0.0 35.3 jit_solution(15332528920466100496)
XLA Ops:
  0.0 0.0 copy-start
  0.0 32.3 %spectra.1 = bf16[5,4,32,8,256]{4,3,2,1,0:T(8,128)(2,1)S(1)} custom-call(bf16[2,4,94208]{2,1,0:T(4,128)(2,1)} %x_hbm.1, f32[16,4096]{1,0:T(8,128)} %taps_hbm.1, bf16[2,256,256]{2,1,0:T(8,128)(2,1)} %constant.8.clone.first_hbm, bf16[2,256,256]{2,1,0:T(8,128)(2,1)} %constant.9.clone.second_hbm, f32[2,32,128]{2,1,0:T(8,128)} %constant.10.clone.turn_hbm), custom_call_target="tpu_custom_call" | custom-call | tf_op jit(solution)/shard_map/spectra/pallas_call | solution.py:241
  32.3 0.0 copy-done
  32.3 3.0 %correlate.1 = f32[2,4,1024,128]{3,2,1,0:T(8,128)} custom-call(bf16[5,4,256,256]{3,2,1,0:T(8,128)(2,1)S(1)} %bitcast.4, bf16[256,256]{1,0:T(8,128)(2,1)S(1)} %copy-done), custom_call_target="tpu_custom_call" | custom-call | tf_op jit(solution)/shard_map/correlate/pallas_call | solution.py:295
Async XLA Ops:
  0.0 32.3 %copy-start = (bf16[256,256]{1,0:T(8,128)(2,1)S(1)}, bf16[256,256]{1,0:T(8,128)(2,1)}, u32[]{:S(2)}) copy-start(bf16[256,256]{1,0:T(8,128)(2,1)} %constant.11.clone.sort_ref) | copy-start | bytes 393220

commit v6 on v5

--- a/solution.py
+++ b/solution.py
@@ -20,7 +20,7 @@
 OWNED = 4
 GROUPS = 32
 N_SHIFTS = GROUPS - 1
-LOADS = 2
+LOADS = 4
 SPAN = CHANNELS // LOADS
 KEPT = FRAMES * SLOW
 ROWS = 2 * WIDTH
@@ -95,7 +95,7 @@
 
     for group in range(LOADS):
         ready(group)
-        lax.fori_loop(0, SPAN // FAST, functools.partial(column, group), 0, unroll=4)
+        lax.fori_loop(0, SPAN // FAST, functools.partial(column, group), 0, unroll=8)
     tables_ready()
     high, low = split(fir[...])
     dot = functools.partial(jnp.dot, preferred_element_type=F32)

time: 35.4 us -> 35.5 us (level)
  no operation moved by 1% of the time
where the time goes in v6:
time: 35.5 us; the launch traced here: 35.4 us
  Pallas kernels  35.4 us (100%)
    pallas_call x1, Pallas kernels, spread_spectra(): pl.pallas_call(spectra_kernel, out_shape=jax.ShapeDtypeStruct((N_BCOL + 1...  32.4 us
    pallas_call x1, Pallas kernels, correlate(): pl.pallas_call(correlate_kernel, out_shape=jax.ShapeDtypeStruct(shape, F3...  2.99 us

profile of v6, /device:TPU:2, one launch (start us, length us, event | category | flops | bytes accessed | tf_op | source)
XLA Modules:
  0.0 35.4 jit_solution(3588922731271082359)
XLA Ops:
  0.0 0.0 copy-start
  0.0 32.4 %spectra.1 = bf16[5,4,32,8,256]{4,3,2,1,0:T(8,128)(2,1)S(1)} custom-call(bf16[2,4,94208]{2,1,0:T(4,128)(2,1)} %x_hbm.1, f32[16,4096]{1,0:T(8,128)} %taps_hbm.1, bf16[2,256,256]{2,1,0:T(8,128)(2,1)} %constant.8.clone.first_hbm, bf16[2,256,256]{2,1,0:T(8,128)(2,1)} %constant.9.clone.second_hbm, f32[2,32,128]{2,1,0:T(8,128)} %constant.10.clone.turn_hbm), custom_call_target="tpu_custom_call" | custom-call | tf_op jit(solution)/shard_map/spectra/pallas_call | solution.py:241
  32.4 0.0 copy-done
  32.4 3.0 %correlate.1 = f32[2,4,1024,128]{3,2,1,0:T(8,128)} custom-call(bf16[5,4,256,256]{3,2,1,0:T(8,128)(2,1)S(1)} %bitcast.4, bf16[256,256]{1,0:T(8,128)(2,1)S(1)} %copy-done), custom_call_target="tpu_custom_call" | custom-call | tf_op jit(solution)/shard_map/correlate/pallas_call | solution.py:295
Async XLA Ops:
  0.0 32.4 %copy-start = (bf16[256,256]{1,0:T(8,128)(2,1)S(1)}, bf16[256,256]{1,0:T(8,128)(2,1)}, u32[]{:S(2)}) copy-start(bf16[256,256]{1,0:T(8,128)(2,1)} %constant.11.clone.sort_ref) | copy-start | bytes 393220
